TPU v7x, 32 devices: a whole 2x2x4 slice. The times are simulated.
32 devices in a mesh: dp: 8 (over z, y), mp: 4 (over x, core).
Axes of the slice: x: 2, y: 2, z: 4, core: 2. Of those that a mesh axis runs over, the one named last changes fastest.
Arguments:
- tokens: bfloat16 [16560, 1024], P('dp'), may hold values from -6 to 6
- offsets: int32 [48, 5], P('dp'), may hold values from 0 to 308, as said below
- first_gain: float32 [1024], replicated, may hold values from 0.1 to 1.9
- first_shift: float32 [1024], replicated, may hold values from -1.8 to 1.8
- qkv_weight: float32 [1024, 3, 1024], P('dp', None, 'mp'), may hold values from -0.1875 to 0.1875
- qv_bias: float32 [2, 1024], P(None, 'mp'), may hold values from -1.8 to 1.8
- proj_weight: float32 [1024, 1024], P('mp', 'dp'), may hold values from -0.5 to 0.5
- proj_bias: float32 [1024], replicated, may hold values from -1.8 to 1.8
- second_gain: float32 [1024], replicated, may hold values from 0.1 to 1.9
- second_shift: float32 [1024], replicated, may hold values from -1.8 to 1.8
- expand_weight: float32 [1024, 4096], P('dp', 'mp'), may hold values from -0.1875 to 0.1875
- expand_bias: float32 [4096], P('mp'), may hold values from -1.8 to 1.8
- shrink_weight: float32 [4096, 1024], P('mp', 'dp'), may hold values from -0.09375 to 0.09375
- shrink_bias: float32 [1024], replicated, may hold values from -1.8 to 1.8
- cotangent: bfloat16 [16560, 1024], P('dp'), may hold values from -6 to 6
Outputs:
- out: bfloat16 [16560, 1024], P('dp')
- d_tokens: float32 [16560, 1024], P('dp')
- d_first_gain: float32 [1024], replicated
- d_first_shift: float32 [1024], replicated
- d_qkv_weight: float32 [1024, 3, 1024], P('dp', None, 'mp')
- d_qv_bias: float32 [2, 1024], P(None, 'mp')
- d_proj_weight: float32 [1024, 1024], P('mp', 'dp')
- d_proj_bias: float32 [1024], replicated
- d_second_gain: float32 [1024], replicated
- d_second_shift: float32 [1024], replicated
- d_expand_weight: float32 [1024, 4096], P('dp', 'mp')
- d_expand_bias: float32 [4096], P('mp')
- d_shrink_weight: float32 [4096, 1024], P('mp', 'dp')
- d_shrink_bias: float32 [1024], replicated
Inputs may be any that keep to these rules, and one draw needn't show every extreme that they name: `offsets`: each row lists, rising, where the 5 crops of one crop set start within its 345 tokens: the first starts at 0, one crop spans 197 tokens, the others 37 each, and the last ends at the set's end.
All inputs are finite; a program needn't handle non-finite values.
Results may differ from a plain program's by a relative error of at most 0.015.
Values may be sent and summed in bfloat16 or wider, within the bound.
No kernel may reach another device: no remote copies, remote signals or barrier semaphores. Data moves between devices by JAX's collectives and lax.ppermute only.
A program may use at most 128 MiB of HBM per device.

v0:
```python
import jax
import jax.numpy as jnp
from jax import lax
from jax.sharding import PartitionSpec as P

HEAD_DIM = 64
SET_TOKENS = 345
norm_eps = 1e-06
masked_score = -1e30
root_half = 0.7071067811865476


def layer_norm(values, gain, shift):
    centre = jnp.mean(values, axis=-1, keepdims=True)
    offset_rows = values - centre
    spread = jnp.mean(offset_rows * offset_rows, axis=-1, keepdims=True)
    return offset_rows * lax.rsqrt(spread + norm_eps) * gain + shift


def normalized(values):
    centre = jnp.mean(values, axis=-1, keepdims=True)
    offset_rows = values - centre
    spread = jnp.mean(offset_rows * offset_rows, axis=-1, keepdims=True)
    return offset_rows * lax.rsqrt(spread + norm_eps)


def gelu(values):
    return 0.5 * values * (1.0 + lax.erf(values * root_half))


def matmul(left, right):
    return jnp.dot(left, right, preferred_element_type=jnp.float32)


def set_scores(query_rows, key_rows, crop_ids, factor):
    scores = (
        jnp.einsum("qhe,khe->hqk", query_rows, key_rows, preferred_element_type=jnp.float32)
        * factor
    )
    same_crop = crop_ids[:, None] == crop_ids[None, :]
    return jnp.where(same_crop[None], scores, masked_score)


def attend_forward(factor):

    def attend(pieces):
        query_rows, key_rows, value_rows, crop_ids = pieces
        scores = set_scores(query_rows, key_rows, crop_ids, factor)
        peak_score = jnp.max(scores, axis=-1, keepdims=True)
        raised = jnp.exp(scores - peak_score)
        row_total = jnp.sum(raised, axis=-1, keepdims=True)
        weights = (raised / row_total).astype(jnp.bfloat16)
        mixed = jnp.einsum("hqk,khe->qhe", weights, value_rows, preferred_element_type=jnp.float32)
        return (mixed.astype(jnp.bfloat16), (peak_score + jnp.log(row_total))[..., 0])

    return attend


def attend_backward(factor):

    def backward(pieces):
        query_rows, key_rows, value_rows, crop_ids, log_total, grad_mixed = pieces
        scores = set_scores(query_rows, key_rows, crop_ids, factor)
        weights = jnp.exp(scores - log_total[..., None])
        grad_values = jnp.einsum(
            "hqk,qhe->khe",
            weights.astype(jnp.bfloat16),
            grad_mixed,
            preferred_element_type=jnp.float32,
        )
        grad_weights = jnp.einsum(
            "qhe,khe->hqk", grad_mixed, value_rows, preferred_element_type=jnp.float32
        )
        grad_scores = weights * (
            grad_weights - jnp.sum(weights * grad_weights, axis=-1, keepdims=True)
        )
        scores_low = grad_scores.astype(jnp.bfloat16)
        grad_queries = (
            jnp.einsum("hqk,khe->qhe", scores_low, key_rows, preferred_element_type=jnp.float32)
            * factor
        )
        grad_keys = (
            jnp.einsum("hqk,qhe->khe", scores_low, query_rows, preferred_element_type=jnp.float32)
            * factor
        )
        return (grad_queries, grad_keys, grad_values)

    return backward


def shards(
    tokens,
    offsets,
    first_gain,
    first_shift,
    qkv_weight,
    qv_bias,
    proj_weight,
    proj_bias,
    second_gain,
    second_shift,
    expand_weight,
    expand_bias,
    shrink_weight,
    shrink_bias,
    cotangent,
):
    row_count = tokens.shape[0]
    sets_here = offsets.shape[0]
    width_here = qkv_weight.shape[2]
    local_heads = width_here // HEAD_DIM
    factor = HEAD_DIM ** (-0.5)
    model_count = lax.axis_size("mp")
    model_index = lax.axis_index("mp")
    extra = -row_count % model_count
    share_rows = (row_count + extra) // model_count
    share_start = model_index * share_rows
    row_numbers = jnp.arange(row_count, dtype=jnp.int32)
    row_mask = ((row_numbers >= share_start) & (row_numbers < share_start + share_rows)).astype(
        jnp.float32
    )[:, None]
    positions = jnp.arange(SET_TOKENS, dtype=jnp.int32)
    crop_ids = jnp.sum((positions[None, :, None] >= offsets[:, None, :]).astype(jnp.int32), axis=-1)
    qkv_master = qkv_weight.astype(jnp.bfloat16)
    proj_master = proj_weight.astype(jnp.bfloat16)
    expand_master = expand_weight.astype(jnp.bfloat16)
    shrink_master = shrink_weight.astype(jnp.bfloat16)
    qkv_full, proj_full, expand_full, shrink_full = (
        lax.all_gather(qkv_master, "dp", axis=0, tiled=True),
        lax.all_gather(proj_master, "dp", axis=1, tiled=True),
        lax.all_gather(expand_master, "dp", axis=0, tiled=True),
        lax.all_gather(shrink_master, "dp", axis=1, tiled=True),
    )
    inputs = tokens.astype(jnp.float32)
    first_low = layer_norm(inputs, first_gain, first_shift).astype(jnp.bfloat16)
    projected = jnp.einsum("td,dcf->tcf", first_low, qkv_full, preferred_element_type=jnp.float32)
    shaped = (sets_here, SET_TOKENS, local_heads, HEAD_DIM)
    query_rows = (projected[:, 0] + qv_bias[0]).astype(jnp.bfloat16).reshape(shaped)
    key_rows = projected[:, 1].astype(jnp.bfloat16).reshape(shaped)
    value_rows = (projected[:, 2] + qv_bias[1]).astype(jnp.bfloat16).reshape(shaped)
    attended, log_total = lax.map(
        attend_forward(factor), (query_rows, key_rows, value_rows, crop_ids)
    )
    attended_flat = attended.reshape(row_count, width_here)
    attn_part = matmul(attended_flat, proj_full)
    residual = inputs + lax.psum(attn_part, "mp") + proj_bias
    second_low = layer_norm(residual, second_gain, second_shift).astype(jnp.bfloat16)
    hidden_pre = matmul(second_low, expand_full) + expand_bias
    hidden = gelu(hidden_pre).astype(jnp.bfloat16)
    mlp_part = matmul(hidden, shrink_full)
    outputs = (
        residual + lax.psum(mlp_part.astype(jnp.bfloat16), "mp").astype(jnp.float32) + shrink_bias
    ).astype(jnp.bfloat16)
    grad_out = cotangent.astype(jnp.float32)
    shrink_grad = jnp.einsum("tf,td->fd", hidden, cotangent, preferred_element_type=jnp.float32)
    grad_hidden = jnp.einsum(
        "td,fd->tf", cotangent, shrink_full, preferred_element_type=jnp.float32
    )
    _, gelu_pull = jax.vjp(gelu, hidden_pre)
    grad_pre = gelu_pull(grad_hidden)[0]
    expand_bias_grad = jnp.sum(grad_pre, axis=0)
    grad_pre_low = grad_pre.astype(jnp.bfloat16)
    expand_grad = jnp.einsum(
        "td,tf->df", second_low, grad_pre_low, preferred_element_type=jnp.float32
    )
    second_part = jnp.einsum(
        "tf,df->td", grad_pre_low, expand_full, preferred_element_type=jnp.float32
    )
    grad_second = lax.psum(second_part, "mp")
    _, second_pull = jax.vjp(lambda values: layer_norm(values, second_gain, second_shift), residual)
    grad_residual = second_pull(grad_second)[0] + grad_out
    grad_second_kept = grad_second * row_mask
    second_gain_grad = jnp.sum(grad_second_kept * normalized(residual), axis=0)
    second_shift_grad = jnp.sum(grad_second_kept, axis=0)
    proj_bias_grad = jnp.sum(grad_residual * row_mask, axis=0)
    shrink_bias_grad = jnp.sum(grad_out * row_mask, axis=0)
    residual_low = grad_residual.astype(jnp.bfloat16)
    proj_grad = jnp.einsum(
        "tc,td->cd", attended_flat, residual_low, preferred_element_type=jnp.float32
    )
    grad_attended = jnp.einsum(
        "td,cd->tc", residual_low, proj_full, preferred_element_type=jnp.float32
    ).astype(jnp.bfloat16)
    grad_queries, grad_keys, grad_values = lax.map(
        attend_backward(factor),
        (query_rows, key_rows, value_rows, crop_ids, log_total, grad_attended.reshape(shaped)),
    )
    grad_queries = grad_queries.reshape(row_count, width_here)
    grad_keys = grad_keys.reshape(row_count, width_here)
    grad_values = grad_values.reshape(row_count, width_here)
    qv_bias_grad = jnp.stack([jnp.sum(grad_queries, axis=0), jnp.sum(grad_values, axis=0)])
    grad_projected = jnp.stack([grad_queries, grad_keys, grad_values], axis=1).astype(jnp.bfloat16)
    qkv_grad = jnp.einsum(
        "td,tcf->dcf", first_low, grad_projected, preferred_element_type=jnp.float32
    )
    first_part = jnp.einsum(
        "tcf,dcf->td", grad_projected, qkv_full, preferred_element_type=jnp.float32
    )
    grad_first = lax.psum(first_part.astype(jnp.bfloat16), "mp").astype(jnp.float32)
    _, first_pull = jax.vjp(lambda values: layer_norm(values, first_gain, first_shift), inputs)
    grad_tokens = first_pull(grad_first)[0] + grad_residual
    grad_first_kept = grad_first * row_mask
    first_gain_grad = jnp.sum(grad_first_kept * normalized(inputs), axis=0)
    first_shift_grad = jnp.sum(grad_first_kept, axis=0)
    qkv_part, proj_part, expand_part, shrink_part = (
        lax.psum_scatter(
            qkv_grad.astype(jnp.bfloat16), "dp", scatter_dimension=0, tiled=True
        ).astype(jnp.float32),
        lax.psum_scatter(
            proj_grad.astype(jnp.bfloat16), "dp", scatter_dimension=1, tiled=True
        ).astype(jnp.float32),
        lax.psum_scatter(
            expand_grad.astype(jnp.bfloat16), "dp", scatter_dimension=0, tiled=True
        ).astype(jnp.float32),
        lax.psum_scatter(
            shrink_grad.astype(jnp.bfloat16), "dp", scatter_dimension=1, tiled=True
        ).astype(jnp.float32),
    )
    qv_part, expand_bias_part = lax.psum((qv_bias_grad, expand_bias_grad), "dp")
    small_parts = lax.psum(
        (
            first_gain_grad,
            first_shift_grad,
            proj_bias_grad,
            second_gain_grad,
            second_shift_grad,
            shrink_bias_grad,
        ),
        ("dp", "mp"),
    )
    return (
        outputs,
        grad_tokens,
        small_parts[0],
        small_parts[1],
        qkv_part,
        qv_part,
        proj_part,
        small_parts[2],
        small_parts[3],
        small_parts[4],
        expand_part,
        expand_bias_part,
        shrink_part,
        small_parts[5],
    )


def solution(mesh):
    placed = (
        P("dp", None),
        P("dp", None),
        P(),
        P(),
        P("dp", None, "mp"),
        P(None, "mp"),
        P("mp", "dp"),
        P(),
        P(),
        P(),
        P("dp", "mp"),
        P("mp"),
        P("mp", "dp"),
        P(),
        P("dp", None),
    )
    return jax.shard_map(
        shards,
        mesh=mesh,
        in_specs=placed,
        out_specs=(
            P("dp", None),
            P("dp", None),
            P(),
            P(),
            P("dp", None, "mp"),
            P(None, "mp"),
            P("mp", "dp"),
            P(),
            P(),
            P(),
            P("dp", "mp"),
            P("mp"),
            P("mp", "dp"),
            P(),
        ),
        check_vma=False,
    )
```

profile of v0, /device:TPU:0, one launch (start us, length us, event | category | flops | bytes accessed | tf_op | source)
XLA Modules:
  0.0 1080.6 jit_solution(10375636445222786847)
XLA Ops:
  16.9 34.5 %all_gather.13 = bf16[256,1024]{1,0:T(8,128)(2,1)} all-gather(bf16[256,128]{1,0:T(8,128)(2,1)S(1)} %convert_element_type.121), channel_id=1, replica_groups=mesh['dp'=8,'mp'=4] {'dp'}, dimensions={1}, use_global_device_ids=true | all-gather | bytes 589824 | tf_op jit(solution)/shard_map/all_gather | solution.py:130
  51.4 10.1 all-gather.4.cloned.1.call-done
  94.1 20.2 %while.26 = (s32[]{:T(128)}, bf16[6,345,4,64]{1,3,2,0:T(8,128)(2,1)}, f32[6,4,345]{2,1,0:T(4,128)}, bf16[6,345,4,64]{1,3,2,0:T(8,128)(2,1)S(1)}, s32[6,345]{1,0:...) while((s32[]{:T(128)}, ...), condition=%wide.region_6.7_spmd, body=%wide.region_3.6_spmd.sunk | while | flops 127800768 | bytes 7318627 | solution.py:141
  130.2 151.0 %all-reduce.7.cloned.1.call-done = f32[2070,1024]{1,0:T(8,128)} async-done(((f32[2070,1024]{1,0:T(8,128)}), f32[2070,1024]{1,0:T(8,128)}) %all-reduce.7.cloned.1.call-update) | async-done | bytes 8478736 | tf_op jit(solution)/shard_map/psum | solution.py:146
  293.3 40.2 %all-gather.6.cloned.1.call-done = bf16[1024,1024]{1,0:T(8,128)(2,1)} async-done(((bf16[128,1024]{1,0:T(8,128)(2,1)}), bf16[1024,1024]{1,0:T(8,128)(2,1)}) %all-gather.6.cloned.1.call-update) | async-done | bytes 2097168 | tf_op jit(solution)/shard_map/all_gather | solution.py:131
  333.5 10.9 %fusion.88 = f32[2070,1024]{1,0:T(8,128)} fusion(bf16[2070,1024]{1,0:T(8,128)(2,1)} %add_convert_fusion.1, bf16[1024,1024]{1,0:T(8,128)(2,1)} %all-gather.6.cloned.1.call-done), kind=kOutput, calls=%fused_computation.143 | convolution fusion | flops 4341104640 | bytes 14815232 | tf_op jit(solution)/shard_map/dot_general | solution.py:32
  344.4 41.4 %all-gather.8.cloned.1.call-done = bf16[1024,1024]{1,0:T(8,128)(2,1)} async-done(((bf16[1024,128]{1,0:T(8,128)(2,1)}), bf16[1024,1024]{1,0:T(8,128)(2,1)}) %all-gather.8.cloned.1.call-update) | async-done | bytes 2097168 | tf_op jit(solution)/shard_map/all_gather | solution.py:132
  385.8 13.9 %fusion.80 = (f32[1024]{0:T(1024)}, bf16[2070,1024]{1,0:T(8,128)(2,1)S(1)}, bf16[2070,1024]{1,0:T(8,128)(2,1)}) fusion(f32[2070,1024]{1,0:T(8,128)} %fusion.88, f32[1024]{0:T(1024)S(1)} %copy-done.29, bf16[2070,1024]{1,0:T(8,128)(2,1)} %param.33, bf16[1024,1024]{1,0:T(8,128)(2,1)} %all-gather.8.cloned.1.call-done), kind=kOutput, calls=%fused_computation.136 | convolution fusion | flops 4377138176 | bytes 23302144 | tf_op jit(solution)/shard_map/td,fd->tf/dot_general | solution.py:156
  401.7 7.2 fusion.65
  408.9 9.5 convolution_convert_fusion.3
  422.5 9.2 fusion.67
  431.7 130.3 %all-reduce.9.cloned.1.call-done = f32[2070,1024]{1,0:T(8,128)} async-done(((f32[2070,1024]{1,0:T(8,128)}), f32[2070,1024]{1,0:T(8,128)}) %all-reduce.9.cloned.1.call-update) | async-done | bytes 8478736 | tf_op jit(solution)/shard_map/psum | solution.py:169
  562.0 8.2 multiply_reduce_fusion.1
  587.3 46.0 %while.27 = (s32[]{:T(128)}, f32[6,345,4,64]{1,3,2,0:T(8,128)}, bf16[6,345,4,64]{1,3,2,0:T(8,128)(2,1)}, f32[6,345,4,64]{1,3,2,0:T(8,128)}, bf16[6,345,4,64]{1,3...) while((s32[]{:T(128)}, f32[6,345,4,64]{1,3,2,0:T(8,128)}, ...), condition=%wide.region_16.17_spmd, body=%wide.region_14.16_spmd.sunk | while | flops 309283200 | bytes 17905568 | solution.py:184
  668.8 9.3 convolution_convert_fusion.4
  678.3 9.7 convolution_convert_fusion.1
  695.0 8.4 reduce-scatter.11.cloned.1.call-done
  705.5 20.3 %all-reduce.1 = (f32[2,256]{1,0:T(2,128)}, f32[1024]{0:T(1024)}) all-reduce(f32[2,256]{1,0:T(2,128)S(1)} %pad_maximum_fusion, f32[1024]{0:T(1024)S(1)} %copy-done.25), channel_id=1, replica_groups=mesh['dp'=8,'mp'=4] {'dp'}, use_global_device_ids=true, to_apply=%region_27.28 | all-reduce | flops 1536 | bytes 12288 | tf_op jit(solution)/shard_map/psum | solution.py:219
  725.7 42.0 %reduce-scatter.13.cloned.1.call-done = bf16[128,256]{1,0:T(8,128)(2,1)} async-done(((bf16[1024,256]{1,0:T(8,128)(2,1)}), bf16[128,256]{1,0:T(8,128)(2,1)}) %reduce-scatter.13.cloned.1.call-update) | async-done | bytes 65552
  769.4 66.7 %reduce-scatter.9.cloned.1.call-done = bf16[128,3,256]{2,0,1:T(8,128)(2,1)} async-done(((bf16[1024,3,256]{2,0,1:T(8,128)(2,1)}), bf16[128,3,256]{2,0,1:T(8,128)(2,1)}) %reduce-scatter.9.cloned.1.call-update) | async-done | bytes 196624 | tf_op jit(solution)/shard_map/reduce_scatter | solution.py:206
  837.8 155.5 %all-reduce.11.cloned.1.call-done = (bf16[2070,1024]{1,0:T(8,128)(2,1)}, bf16[2070,1024]{1,0:T(8,128)(2,1)}) async-done(((bf16[2070,1024]{1,0:T(8,128)(2,1)}, bf16[2070,1024]{1,0:T(8,128)(2,1)}), (bf16[2070,1024]{1,0:T(8,128)(2,1)}, bf16[2070,1024]{1,0:T(8,128)(2,1)})) %all-reduce.11.cloned.1.call-update) | async-done | bytes 8478736 | tf_op jit(solution)/shard_map/psum | solution.py:152
  998.8 13.9 %fusion.54 = (f32[1024]{0:T(1024)S(1)}, f32[1024]{0:T(1024)S(1)}, f32[1024]{0:T(1024)S(1)}, f32[2070]{0:T(1024)S(1)}, f32[1024]{0:T(1024)S(1)}) fusion(bf16[2070,1024]{1,0:T(8,128)(2,1)} %param.33, f32[2070]{0:T(1024)S(1)} %copy-done.15, f32[2070,1024]{1,0:T(8,128)} %copy-done.2, f32[2070]{0:T(1024)S(1)} %negate_multiply_fusion.1, ...), kind=kLoop, calls=%fused_computation.79 | loop fusion | flops 44507112 | bytes 21266960 | tf_op jit(solution)/shard_map/reduce_sum | solution.py:176
  1012.7 13.7 %add_add_fusion.2 = f32[2070,1024]{1,0:T(8,128)} fusion(bf16[2070,1024]{1,0:T(8,128)(2,1)} %param.19, bf16[2070,1024]{1,0:T(8,128)(2,1)} %get-tuple-element.235, f32[2070]{0:T(1024)S(1)} %negate_multiply_fusion, f32[2070]{0:T(1024)S(1)} %multiply_multiply_fusion, f32[1024]{0:T(1024)S(1)} %copy-done.21, f32[2070]{0:T(1024)S(1)} %copy-done.13, ...), kind=kLoop, calls=%fused_computation.86 | loop fusion | flops 27555840 | bytes 29721016 | tf_op jit(solution)/shard_map/add | solution.py:201
  1033.5 40.0 %all-reduce = (f32[1024]{0:T(1024)}, f32[1024]{0:T(1024)}, f32[1024]{0:T(1024)}, f32[1024]{0:T(1024)}, f32[1024]{0:T(1024)}, /*index=5*/f32[1024]{0:T(1024)}) all-reduce(f32[1024]{0:T(1024)S(1)} %get-tuple-element.189, f32[1024]{0:T(1024)S(1)} %get-tuple-element.187, ...), channel_id=1, replica_groups=mesh['dp'=8,'mp'=4] {'dp','mp'}, use_global_device_ids=true, to_apply=%region_21.22 | all-reduce | flops 6144 | bytes 49152 | tf_op jit(solution)/shard_map/psum | solution.py:220
  (260 shorter events, 219.5 us)
Async XLA Ops:
  7.2 54.3 %all-gather.4.cloned.1.call-start = ((), (), s32[]{:S(2)}) async-start(), calls=%async_computation.4 | async-start | bytes 1769472 | tf_op jit(solution)/shard_map/all_gather | solution.py:129
  8.9 272.3 %all-reduce.7.cloned.1.call-start = ((), (), s32[]{:S(2)}) async-start(), calls=%async_computation.5 | async-start | bytes 16973824 | tf_op jit(solution)/shard_map/psum | solution.py:146
  11.9 49.6 %copy-start.20 = (f32[1024]{0:T(1024)S(1)}, f32[1024]{0:T(1024)}, u32[]{:S(2)}) copy-start(f32[1024]{0:T(1024)} %param.21) | copy-start | bytes 12292
  11.9 49.6 %copy-start.30 = (f32[1024]{0:T(1024)S(1)}, f32[1024]{0:T(1024)}, u32[]{:S(2)}) copy-start(f32[1024]{0:T(1024)} %param.22) | copy-start | bytes 12292
  15.0 53.0 %copy-start.10 = (f32[2070]{0:T(1024)}, f32[2070]{0:T(1024)S(1)}, u32[]{:S(2)}) copy-start(f32[2070]{0:T(1024)S(1)} %broadcast_multiply_fusion.1) | copy-start | bytes 24844
  16.9 51.1 %copy-start.12 = (f32[2070]{0:T(1024)}, f32[2070]{0:T(1024)S(1)}, u32[]{:S(2)}) copy-start(f32[2070]{0:T(1024)S(1)} %fusion.78) | copy-start | bytes 24844
  114.3 13.1 %copy-start.18 = (s32[6,345]{1,0:T(8,128)}, s32[6,345]{1,0:T(8,128)S(1)}, u32[]{:S(2)}) copy-start(s32[6,345]{1,0:T(8,128)S(1)} %get-tuple-element.473) | copy-start | bytes 24844
  127.4 153.9 %copy-start.26 = (f32[1024]{0:T(1024)S(1)}, f32[1024]{0:T(1024)}, u32[]{:S(2)}) copy-start(f32[1024]{0:T(1024)} %param.26) | copy-start | bytes 12292
  127.4 206.1 %all-gather.6.cloned.1.call-start = ((), (), s32[]{:S(2)}) async-start(), calls=%async_computation.6 | async-start | bytes 2359296 | tf_op jit(solution)/shard_map/all_gather | solution.py:131
  129.2 256.6 %all-gather.8.cloned.1.call-start = ((), (), s32[]{:S(2)}) async-start(), calls=%async_computation.7 | async-start | bytes 2359296 | tf_op jit(solution)/shard_map/all_gather | solution.py:132
  130.0 432.0 %all-reduce.9.cloned.1.call-start = ((), (), s32[]{:S(2)}) async-start(), calls=%async_computation.8 | async-start | bytes 16973824 | tf_op jit(solution)/shard_map/psum | solution.py:169
  293.3 92.5 %copy-start.29 = (f32[1024]{0:T(1024)S(1)}, f32[1024]{0:T(1024)}, u32[]{:S(2)}) copy-start(f32[1024]{0:T(1024)} %param.30) | copy-start | bytes 12292
  385.8 15.9 %copy-start.27 = (bf16[1024,1024]{1,0:T(8,128)(2,1)S(1)}, bf16[1024,1024]{1,0:T(8,128)(2,1)}, u32[]{:S(2)}) copy-start(bf16[1024,1024]{1,0:T(8,128)(2,1)} %all-gather.6.cloned.1.call-done) | copy-start | bytes 6291460
  408.8 284.2 %reduce-scatter.15.cloned.1.call-start = ((), (), s32[]{:S(2)}) async-start(), calls=%async_computation.12 | async-start | bytes 2359296
  422.4 281.1 %reduce-scatter.11.cloned.1.call-start = ((), (), s32[]{:S(2)}) async-start(), calls=%async_computation.10 | async-start | bytes 2359296 | tf_op jit(solution)/shard_map/reduce_scatter | solution.py:212
  422.5 139.5 %copy-start.14 = (f32[2070]{0:T(1024)}, f32[2070]{0:T(1024)S(1)}, u32[]{:S(2)}) copy-start(f32[2070]{0:T(1024)S(1)} %fusion.77) | copy-start | bytes 24844
  431.7 336.1 %reduce-scatter.13.cloned.1.call-start = ((), (), s32[]{:S(2)}) async-start(), calls=%async_computation.11 | async-start | bytes 589824
  562.0 17.4 %slice-start = ((s8[4243456]{0:T(1024)(128)(4,1)}), s8[4194304]{0:T(1024)(128)(4,1)S(1)}, s32[]{:S(2)}) async-start(s8[4243456]{0:T(1024)(128)(4,1)} %bitcast.139), calls=%async_computation.14 | async-start | bytes 8388608
  665.4 170.7 %reduce-scatter.9.cloned.1.call-start = ((), (), s32[]{:S(2)}) async-start(), calls=%async_computation.9 | async-start | bytes 1769472 | tf_op jit(solution)/shard_map/reduce_scatter | solution.py:206
  678.2 315.1 %all-reduce.11.cloned.1.call-start = ((), (), s32[]{:S(2)}) async-start(), calls=%async_computation.13 | async-start | bytes 16973824 | tf_op jit(solution)/shard_map/psum | solution.py:152
  693.0 12.4 %copy-start.25 = (f32[1024]{0:T(1024)S(1)}, f32[1024]{0:T(1024)}, u32[]{:S(2)}) copy-start(f32[1024]{0:T(1024)} %get-tuple-element.236) | copy-start | bytes 12292
  998.8 27.6 %slice-start.2 = ((s8[4243456]{0:T(1024)(128)(4,1)}), s8[49152]{0:T(1024)(128)(4,1)S(1)}, s32[]{:S(2)}) async-start(s8[4243456]{0:T(1024)(128)(4,1)} %bitcast.142), calls=%async_computation.16 | async-start | bytes 98304
  1012.7 13.7 %slice-start.3 = ((s8[4243456]{0:T(1024)(128)(4,1)}), s8[4194304]{0:T(1024)(128)(4,1)S(1)}, s32[]{:S(2)}) async-start(s8[4243456]{0:T(1024)(128)(4,1)} %bitcast.142), calls=%async_computation.17 | async-start | bytes 8388608
  1012.7 13.7 %copy-start.24 = (f32[1024]{0:T(1024)S(1)}, f32[1024]{0:T(1024)}, u32[]{:S(2)}) copy-start(f32[1024]{0:T(1024)} %param.32) | copy-start | bytes 12292
  (23 other events, 127.0 us)
Sparse Core Ops, SparseCore 0:
  10.8 50.6 all-gather.3
  127.6 153.6 all-reduce.6
  284.2 49.2 all-gather.5
  336.2 49.5 all-gather.7
  409.0 152.9 all-reduce.8
  565.4 67.6 reduce-scatter.14
  636.6 66.8 reduce-scatter.10
  706.8 60.8 reduce-scatter.12
  771.6 64.4 reduce-scatter.8
  839.1 154.1 all-reduce.10
where the time goes:
time: 1080 us
  waiting for transfers between devices  646 us (60%)
  matrix products  143 us (13%)
  other arithmetic  95.7 us (9%)
  blocking collectives  94.8 us (9%)
  local copies, waits for them, and re-layouts  85.2 us (8%)
  between operations  15 us (1%)
    psum x1, waiting for transfers between devices, shards(): lax.psum(mlp_part.astype(jnp.bfloat16), 'mp').astype(jnp.float32)  156 us
    psum x1, waiting for transfers between devices, shards(): residual = inputs + lax.psum(attn_part, 'mp') + proj_bias  151 us
    psum x1, waiting for transfers between devices, shards(): grad_second = lax.psum(second_part, 'mp')  130 us
    reduce_scatter x1, waiting for transfers between devices, shards(): lax.psum_scatter(qkv_grad.astype(jnp.bfloat16), 'dp', scatter_dimension=0...  66.7 us
    unnamed x12, waiting for transfers between devices  42.2 us
    all_gather x1, waiting for transfers between devices, shards(): lax.all_gather(shrink_master, 'dp', axis=1, tiled=True)  41.4 us
    all_gather x1, waiting for transfers between devices, shards(): lax.all_gather(expand_master, 'dp', axis=0, tiled=True)  40.2 us
    psum x1, blocking collectives, shards(): lax.psum((first_gain_grad, first_shift_grad, proj_bias_grad, second_gain_...  40 us
  transfers between devices with their start and end apart: 10, of which 9 were waited for; matrix products, arithmetic and copies ran while one was open for 17% of the time, Pallas kernels for 0%

commit v1 on v0

--- a/solution.py
+++ b/solution.py
@@ -8,6 +8,27 @@
 norm_eps = 1e-06
 masked_score = -1e30
 root_half = 0.7071067811865476
+
+
+def in_order(tiles, dim):
+    shape = list(tiles.shape[1:])
+    shape[dim] *= tiles.shape[0]
+    return jnp.moveaxis(tiles, 0, dim).reshape(shape)
+
+
+def doubled(x, axis):
+    length, index = (lax.axis_size(axis), lax.axis_index(axis))
+    blocks, bit = (x[None], 1)
+    while bit < length:
+        theirs = lax.ppermute(blocks, axis, [(i, i ^ bit) for i in range(length)])
+        low = index & bit == 0
+        blocks = jnp.concatenate([jnp.where(low, blocks, theirs), jnp.where(low, theirs, blocks)])
+        bit *= 2
+    return blocks
+
+
+def gather_by_bits(shard, axis, dim):
+    return in_order(doubled(shard, axis), dim)
 
 
 def layer_norm(values, gain, shift):
@@ -128,7 +149,7 @@
     qkv_full, proj_full, expand_full, shrink_full = (
         lax.all_gather(qkv_master, "dp", axis=0, tiled=True),
         lax.all_gather(proj_master, "dp", axis=1, tiled=True),
-        lax.all_gather(expand_master, "dp", axis=0, tiled=True),
+        gather_by_bits(expand_master, "dp", 0),
         lax.all_gather(shrink_master, "dp", axis=1, tiled=True),
     )
     inputs = tokens.astype(jnp.float32)

time: 1080 us -> 990 us (0.917)
  waiting for transfers between devices: 646 us -> 544 us
    psum x1, waiting for transfers between devices: 151 us -> 69.7 us  [shards(): residual = inputs + lax.psum(attn_part, 'mp') + proj_bias]
    ppermute x0 -> x3, waiting for transfers between devices: none -> 61.3 us  [doubled(): theirs = lax.ppermute(blocks, axis, [(i, i ^ bit) for i in range(length)])]
    all_gather x1, waiting for transfers between devices: 41.4 us -> 0.01 us  [shards(): lax.all_gather(shrink_master, 'dp', axis=1, tiled=True)]
    all_gather x1 -> x0, waiting for transfers between devices: 40.2 us -> none  [shards(): lax.all_gather(expand_master, 'dp', axis=0, tiled=True)]
    unnamed x81 -> x93, local copies, waits for them, and re-layouts: 22.8 us -> 21.3 us
    unnamed x12 -> x11, waiting for transfers between devices: 42.2 us -> 42.1 us
  transfers between devices with their start and end apart: 10 -> 12, of which waited for: 9 -> 10; matrix products, arithmetic and copies ran while one was open for 17% -> 25% of each run, Pallas kernels for 0% -> 0%
where the time goes in v1:
time: 990 us; the launch traced here: 985 us
  waiting for transfers between devices  544 us (55%)
  matrix products  148 us (15%)
  other arithmetic  95.6 us (10%)
  blocking collectives  93.8 us (9%)
  local copies, waits for them, and re-layouts  83 us (8%)
  between operations  14.8 us (1%)
    psum x1, waiting for transfers between devices, shards(): lax.psum(mlp_part.astype(jnp.bfloat16), 'mp').astype(jnp.float32)  156 us
    psum x1, waiting for transfers between devices, shards(): grad_second = lax.psum(second_part, 'mp')  129 us
    psum x1, waiting for transfers between devices, shards(): residual = inputs + lax.psum(attn_part, 'mp') + proj_bias  69.7 us
    reduce_scatter x1, waiting for transfers between devices, shards(): lax.psum_scatter(qkv_grad.astype(jnp.bfloat16), 'dp', scatter_dimension=0...  66.7 us
    ppermute x3, waiting for transfers between devices, doubled(): theirs = lax.ppermute(blocks, axis, [(i, i ^ bit) for i in range(length)])  61.3 us
    unnamed x11, waiting for transfers between devices  42.1 us
    psum x1, blocking collectives, shards(): lax.psum((first_gain_grad, first_shift_grad, proj_bias_grad, second_gain_...  39.9 us
    all_gather x1, blocking collectives, shards(): lax.all_gather(proj_master, 'dp', axis=1, tiled=True)  33.5 us
  transfers between devices with their start and end apart: 12, of which 10 were waited for; matrix products, arithmetic and copies ran while one was open for 25% of the time, Pallas kernels for 0%

profile of v1, /device:TPU:0, one launch (start us, length us, event | category | flops | bytes accessed | tf_op | source)
XLA Modules:
  0.0 985.1 jit_solution(1317291148537597632)
XLA Ops:
  16.6 33.5 %all_gather.10 = bf16[256,1024]{1,0:T(8,128)(2,1)} all-gather(bf16[256,128]{1,0:T(8,128)(2,1)S(1)} %convert_element_type.121), channel_id=1, replica_groups=mesh['dp'=8,'mp'=4] {'dp'}, dimensions={1}, use_global_device_ids=true | all-gather | bytes 589824 | tf_op jit(solution)/shard_map/all_gather | solution.py:151
  50.2 10.6 %all-gather.3.cloned.1.call-done = bf16[1024,3,256]{2,0,1:T(8,128)(2,1)} async-done(((bf16[128,3,256]{2,0,1:T(8,128)(2,1)}), bf16[1024,3,256]{2,0,1:T(8,128)(2,1)}) %all-gather.3.cloned.1.call-update) | async-done | bytes 1572880 | tf_op jit(solution)/shard_map/all_gather | solution.py:150
  91.7 21.8 %while.26 = (s32[]{:T(128)}, bf16[6,345,4,64]{1,3,2,0:T(8,128)(2,1)S(1)}, f32[6,4,345]{2,1,0:T(4,128)}, bf16[6,345,4,64]{1,3,2,0:T(8,128)(2,1)}, s32[6,345]{1,0:...) while((s32[]{:T(128)}, ...), condition=%wide.region_6.7_spmd, body=%wide.region_3.6_spmd.sunk | while | flops 127800768 | bytes 7319127 | solution.py:162
  135.4 10.6 %collective-permute-done.1 = bf16[2,128,1024]{2,1,0:T(8,128)(2,1)} collective-permute-done((bf16[2,128,1024]{2,1,0:T(8,128)(2,1)S(1)}, bf16[2,128,1024]{2,1,0:T(8,128)(2,1)}, u32[]{:S(2)}, u32[]{:S(2)}) %collective-permute-start.1) | collective-permute-done | bytes 524320 | tf_op jit(solution)/shard_map/ppermute | solution.py:23
  151.0 43.9 %collective-permute-done.2 = bf16[4,128,1024]{2,1,0:T(8,128)(2,1)} collective-permute-done((bf16[4,128,1024]{2,1,0:T(8,128)(2,1)}, bf16[4,128,1024]{2,1,0:T(8,128)(2,1)}, u32[]{:S(2)}, u32[]{:S(2)}) %collective-permute-start.2) | collective-permute-done | bytes 1048608 | tf_op jit(solution)/shard_map/ppermute | solution.py:23
  197.8 11.1 %fusion.88 = f32[2070,1024]{1,0:T(8,128)} fusion(bf16[2070,1024]{1,0:T(8,128)(2,1)} %param.33, bf16[1024,1024]{1,0:T(8,128)(2,1)} %all-gather.5.cloned.1.call-done), kind=kOutput, calls=%fused_computation.153 | convolution fusion | flops 4341104640 | bytes 14815232 | tf_op jit(solution)/shard_map/td,fd->tf/dot_general | solution.py:177
  208.9 69.7 %all-reduce.7.cloned.1.call-done = f32[2070,1024]{1,0:T(8,128)} async-done(((f32[2070,1024]{1,0:T(8,128)}), f32[2070,1024]{1,0:T(8,128)}) %all-reduce.7.cloned.1.call-update) | async-done | bytes 8478736 | tf_op jit(solution)/shard_map/psum | solution.py:167
  288.1 14.3 %fusion.80 = (f32[1024]{0:T(1024)}, bf16[2070,1024]{1,0:T(8,128)(2,1)S(1)}, bf16[2070,1024]{1,0:T(8,128)(2,1)}) fusion(f32[2070,1024]{1,0:T(8,128)} %fusion.88, f32[1024]{0:T(1024)S(1)} %copy-done.34, bf16[1024,1024]{1,0:T(8,128)(2,1)S(1)} %bitcast.147, f32[2070,1024]{1,0:T(8,128)S(1)} %get-tuple-element.241, f32[1024]{0:T(1024)S(1)} %copy-done.35, ...), kind=kOutput, calls=%fused_computation.146 | convolution fusion | flops 4387736576 | bytes 27566256 | tf_op jit(solution)/shard_map/dot_general | solution.py:53
  311.7 9.2 convolution_convert_fusion.3
  325.0 12.1 %fusion.67 = bf16[1024,1024]{1,0:T(8,128)(2,1)} fusion(bf16[2070,1024]{1,0:T(8,128)(2,1)} %copy-done.38, f32[2070,1024]{1,0:T(8,128)} %copy-done, f32[1024]{0:T(1024)S(1)} %copy-done.35, f32[1024]{0:T(1024)S(1)} %copy-done.26, f32[2070]{0:T(1024)S(1)} %fusion.79, f32[2070]{0:T(1024)S(1)} %broadcast_multiply_fusion), kind=kOutput, calls=%fused_computation.111 | convolution fusion | flops 4352751616 | bytes 14839984 | tf_op jit(solution)/shard_map/td,tf->df/dot_general | solution.py:184
  337.6 128.8 %all-reduce.9.cloned.1.call-done = f32[2070,1024]{1,0:T(8,128)} async-done(((f32[2070,1024]{1,0:T(8,128)}), f32[2070,1024]{1,0:T(8,128)}) %all-reduce.9.cloned.1.call-update) | async-done | bytes 8478736 | tf_op jit(solution)/shard_map/psum | solution.py:190
  466.5 8.2 multiply_reduce_fusion.1
  491.8 45.9 %while.27 = (s32[]{:T(128)}, f32[6,345,4,64]{1,3,2,0:T(8,128)}, bf16[6,345,4,64]{1,3,2,0:T(8,128)(2,1)}, f32[6,345,4,64]{1,3,2,0:T(8,128)}, bf16[6,345,4,64]{1,3...) while((s32[]{:T(128)}, f32[6,345,4,64]{1,3,2,0:T(8,128)}, ...), condition=%wide.region_16.17_spmd, body=%wide.region_14.16_spmd.sunk | while | flops 309283200 | bytes 17905560 | solution.py:205
  537.7 7.1 fusion.70
  573.2 9.3 convolution_convert_fusion.4
  582.7 9.6 convolution_convert_fusion.1
  599.3 8.7 reduce-scatter.11.cloned.1.call-done
  610.1 20.3 %all-reduce.1 = (f32[2,256]{1,0:T(2,128)}, f32[1024]{0:T(1024)}) all-reduce(f32[2,256]{1,0:T(2,128)S(1)} %pad_maximum_fusion.3, f32[1024]{0:T(1024)S(1)} %copy-done.29), channel_id=1, replica_groups=mesh['dp'=8,'mp'=4] {'dp'}, use_global_device_ids=true, to_apply=%region_27.28 | all-reduce | flops 1536 | bytes 12288 | tf_op jit(solution)/shard_map/psum | solution.py:240
  630.4 42.0 %reduce-scatter.13.cloned.1.call-done = bf16[128,256]{1,0:T(8,128)(2,1)} async-done(((bf16[1024,256]{1,0:T(8,128)(2,1)}), bf16[128,256]{1,0:T(8,128)(2,1)}) %reduce-scatter.13.cloned.1.call-update) | async-done | bytes 65552
  674.0 66.7 %reduce-scatter.9.cloned.1.call-done = bf16[128,3,256]{2,0,1:T(8,128)(2,1)} async-done(((bf16[1024,3,256]{2,0,1:T(8,128)(2,1)}), bf16[128,3,256]{2,0,1:T(8,128)(2,1)}) %reduce-scatter.9.cloned.1.call-update) | async-done | bytes 196624 | tf_op jit(solution)/shard_map/reduce_scatter | solution.py:227
  742.4 155.7 %all-reduce.11.cloned.1.call-done = (bf16[2070,1024]{1,0:T(8,128)(2,1)}, bf16[2070,1024]{1,0:T(8,128)(2,1)}) async-done(((bf16[2070,1024]{1,0:T(8,128)(2,1)}, bf16[2070,1024]{1,0:T(8,128)(2,1)}), (bf16[2070,1024]{1,0:T(8,128)(2,1)}, bf16[2070,1024]{1,0:T(8,128)(2,1)})) %all-reduce.11.cloned.1.call-update) | async-done | bytes 8478736 | tf_op jit(solution)/shard_map/psum | solution.py:173
  903.5 14.0 %fusion.54 = (f32[1024]{0:T(1024)S(1)}, f32[1024]{0:T(1024)S(1)}, f32[1024]{0:T(1024)S(1)}, f32[2070]{0:T(1024)S(1)}, f32[1024]{0:T(1024)S(1)}) fusion(bf16[2070,1024]{1,0:T(8,128)(2,1)} %param.33, f32[2070]{0:T(1024)S(1)} %copy-done.20, f32[2070,1024]{1,0:T(8,128)} %copy-done.2, f32[2070]{0:T(1024)S(1)} %negate_multiply_fusion.1, ...), kind=kLoop, calls=%fused_computation.79 | loop fusion | flops 44507112 | bytes 21266960 | tf_op jit(solution)/shard_map/reduce_sum | solution.py:197
  917.5 13.7 %add_add_fusion.2 = f32[2070,1024]{1,0:T(8,128)} fusion(bf16[2070,1024]{1,0:T(8,128)(2,1)} %param.19, bf16[2070,1024]{1,0:T(8,128)(2,1)} %get-tuple-element.235, f32[2070]{0:T(1024)S(1)} %negate_multiply_fusion, f32[2070]{0:T(1024)S(1)} %multiply_multiply_fusion, f32[1024]{0:T(1024)S(1)} %copy-done.25, f32[2070]{0:T(1024)S(1)} %copy-done.18, ...), kind=kLoop, calls=%fused_computation.86 | loop fusion | flops 27555840 | bytes 29721016 | tf_op jit(solution)/shard_map/add | solution.py:222
  938.3 39.9 %all-reduce = (f32[1024]{0:T(1024)}, f32[1024]{0:T(1024)}, f32[1024]{0:T(1024)}, f32[1024]{0:T(1024)}, f32[1024]{0:T(1024)}, /*index=5*/f32[1024]{0:T(1024)}) all-reduce(f32[1024]{0:T(1024)S(1)} %get-tuple-element.189, f32[1024]{0:T(1024)S(1)} %get-tuple-element.187, ...), channel_id=1, replica_groups=mesh['dp'=8,'mp'=4] {'dp','mp'}, use_global_device_ids=true, to_apply=%region_21.22 | all-reduce | flops 6144 | bytes 49152 | tf_op jit(solution)/shard_map/psum | solution.py:241
  (280 shorter events, 230.7 us)
Async XLA Ops:
  7.2 53.6 %all-gather.3.cloned.1.call-start = ((), (), s32[]{:S(2)}) async-start(), calls=%async_computation.4 | async-start | bytes 1769472 | tf_op jit(solution)/shard_map/all_gather | solution.py:150
  8.9 188.8 %all-gather.5.cloned.1.call-start = ((), (), s32[]{:S(2)}) async-start(), calls=%async_computation.6 | async-start | bytes 2359296 | tf_op jit(solution)/shard_map/all_gather | solution.py:153
  10.8 267.8 %all-reduce.7.cloned.1.call-start = ((), (), s32[]{:S(2)}) async-start(), calls=%async_computation.5 | async-start | bytes 16973824 | tf_op jit(solution)/shard_map/psum | solution.py:167
  10.9 49.9 %copy-start.24 = (f32[1024]{0:T(1024)S(1)}, f32[1024]{0:T(1024)}, u32[]{:S(2)}) copy-start(f32[1024]{0:T(1024)} %param.21) | copy-start | bytes 12292
  10.9 49.9 %copy-start.36 = (f32[1024]{0:T(1024)S(1)}, f32[1024]{0:T(1024)}, u32[]{:S(2)}) copy-start(f32[1024]{0:T(1024)} %param.22) | copy-start | bytes 12292
  14.3 46.4 %copy-start.14 = (f32[2070]{0:T(1024)}, f32[2070]{0:T(1024)S(1)}, u32[]{:S(2)}) copy-start(f32[2070]{0:T(1024)S(1)} %broadcast_multiply_fusion.1) | copy-start | bytes 24844
  16.2 44.5 %copy-start.17 = (f32[2070]{0:T(1024)}, f32[2070]{0:T(1024)S(1)}, u32[]{:S(2)}) copy-start(f32[2070]{0:T(1024)S(1)} %fusion.78) | copy-start | bytes 24844
  113.5 10.8 %copy-start.23 = (s32[6,345]{1,0:T(8,128)}, s32[6,345]{1,0:T(8,128)S(1)}, u32[]{:S(2)}) copy-start(s32[6,345]{1,0:T(8,128)S(1)} %get-tuple-element.479) | copy-start | bytes 24844
  124.3 342.1 %all-reduce.9.cloned.1.call-start = ((), (), s32[]{:S(2)}) async-start(), calls=%async_computation.7 | async-start | bytes 16973824 | tf_op jit(solution)/shard_map/psum | solution.py:190
  125.4 7.5 collective-permute-start
  133.7 12.3 %collective-permute-start.1 = (bf16[2,128,1024]{2,1,0:T(8,128)(2,1)S(1)}, bf16[2,128,1024]{2,1,0:T(8,128)(2,1)}, u32[]{:S(2)}, u32[]{:S(2)}) collective-permute-start(bf16[2,128,1024]{2,1,0:T(8,128)(2,1)S(1)} %pad_maximum_fusion.2), channel_id=1, source_target_pairs={{0,8},{4,12},{8,0},{12,4},{16,24},{20,28},{24,16},{28,20},{1,9},{5... | collective-permute-start | bytes 1572872 | tf_op jit(solution)/shard_map/ppermute | solution.py:23
  148.3 46.6 %collective-permute-start.2 = (bf16[4,128,1024]{2,1,0:T(8,128)(2,1)}, bf16[4,128,1024]{2,1,0:T(8,128)(2,1)}, u32[]{:S(2)}, u32[]{:S(2)}) collective-permute-start(bf16[4,128,1024]{2,1,0:T(8,128)(2,1)} %pad_maximum_fusion.1), channel_id=1, source_target_pairs={{0,16},{4,20},{8,24},{12,28},{16,0},{20,4},{24,8},{28,12},{1,17},{... | collective-permute-start | bytes 3145736 | tf_op jit(solution)/shard_map/ppermute | solution.py:23
  197.8 80.8 %copy-start.31 = (f32[1024]{0:T(1024)S(1)}, f32[1024]{0:T(1024)}, u32[]{:S(2)}) copy-start(f32[1024]{0:T(1024)} %param.26) | copy-start | bytes 12292
  311.5 285.9 %reduce-scatter.15.cloned.1.call-start = ((), (), s32[]{:S(2)}) async-start(), calls=%async_computation.11 | async-start | bytes 2359296
  324.9 283.2 %reduce-scatter.11.cloned.1.call-start = ((), (), s32[]{:S(2)}) async-start(), calls=%async_computation.9 | async-start | bytes 2359296 | tf_op jit(solution)/shard_map/reduce_scatter | solution.py:233
  325.0 141.5 %copy-start.19 = (f32[2070]{0:T(1024)}, f32[2070]{0:T(1024)S(1)}, u32[]{:S(2)}) copy-start(f32[2070]{0:T(1024)S(1)} %fusion.77) | copy-start | bytes 24844
  337.1 335.2 %reduce-scatter.13.cloned.1.call-start = ((), (), s32[]{:S(2)}) async-start(), calls=%async_computation.10 | async-start | bytes 589824
  466.4 17.4 %slice-start = ((s8[4243456]{0:T(1024)(128)(4,1)}), s8[4194304]{0:T(1024)(128)(4,1)S(1)}, s32[]{:S(2)}) async-start(s8[4243456]{0:T(1024)(128)(4,1)} %bitcast.142), calls=%async_computation.13 | async-start | bytes 8388608
  571.0 169.7 %reduce-scatter.9.cloned.1.call-start = ((), (), s32[]{:S(2)}) async-start(), calls=%async_computation.8 | async-start | bytes 1769472 | tf_op jit(solution)/shard_map/reduce_scatter | solution.py:227
  582.6 315.5 %all-reduce.11.cloned.1.call-start = ((), (), s32[]{:S(2)}) async-start(), calls=%async_computation.12 | async-start | bytes 16973824 | tf_op jit(solution)/shard_map/psum | solution.py:173
  597.3 12.7 %copy-start.29 = (f32[1024]{0:T(1024)S(1)}, f32[1024]{0:T(1024)}, u32[]{:S(2)}) copy-start(f32[1024]{0:T(1024)} %get-tuple-element.236) | copy-start | bytes 12292
  903.5 27.7 %slice-start.2 = ((s8[4243456]{0:T(1024)(128)(4,1)}), s8[49152]{0:T(1024)(128)(4,1)S(1)}, s32[]{:S(2)}) async-start(s8[4243456]{0:T(1024)(128)(4,1)} %bitcast.145), calls=%async_computation.15 | async-start | bytes 98304
  917.5 13.7 %slice-start.3 = ((s8[4243456]{0:T(1024)(128)(4,1)}), s8[4194304]{0:T(1024)(128)(4,1)S(1)}, s32[]{:S(2)}) async-start(s8[4243456]{0:T(1024)(128)(4,1)} %bitcast.145), calls=%async_computation.16 | async-start | bytes 8388608
  917.5 13.7 %copy-start.28 = (f32[1024]{0:T(1024)S(1)}, f32[1024]{0:T(1024)}, u32[]{:S(2)}) copy-start(f32[1024]{0:T(1024)} %param.32) | copy-start | bytes 12292
  (31 other events, 162.8 us)
Sparse Core Ops, SparseCore 0:
  10.8 49.9 all-gather.2
  63.4 50.3 all-gather.4
  124.5 154.0 all-reduce.6
  311.6 154.8 all-reduce.8
  469.8 67.8 reduce-scatter.14
  541.1 66.9 reduce-scatter.10
  611.4 60.8 reduce-scatter.12
  676.2 64.4 reduce-scatter.8
  743.9 154.1 all-reduce.10
